TPU v7x, 256 devices: a whole 4x4x8 slice. The times are simulated.
256 devices in a mesh: member: 4 (over y), seq: 64 (over z, x, core).
Axes of the slice: x: 4, y: 4, z: 8, core: 2. Of those that a mesh axis runs over, the one named last changes fastest.
Arguments:
- hidden: bfloat16 [4, 24576, 2880], P('member', 'seq'), may hold values from -6 to 6
- segments: int32 [24576], replicated, may hold values from 0 to 127, never falling along the last dimension, each value on 1 to 768 neighbouring positions
- pre_gain: float32 [4, 2880], P('member'), may hold values from 0.5 to 1.5
- w_query: bfloat16 [4, 2880, 2048], P('member', 'seq'), may hold values from -3 to 3
- w_key: bfloat16 [4, 2880, 256], P('member', 'seq'), may hold values from -3 to 3
- w_value: bfloat16 [4, 2880, 256], P('member', 'seq'), may hold values from -0.109375 to 0.109375
- w_output: bfloat16 [4, 2048, 2880], P('member', 'seq'), may hold values from -0.125 to 0.125
- post_gain: float32 [4, 2880], P('member'), may hold values from 0.5 to 1.5
- final_gain: float32 [4, 2880], P('member'), may hold values from 0.5 to 1.5
- w_judge: bfloat16 [4, 2880, 128], P('member'), may hold values from -0.21875 to 0.21875
Outputs:
- residual_out: bfloat16 [4, 24576, 2880], P('member', 'seq')
- logits: float32 [24576, 128], P('seq')
Inputs may be any that keep to these rules, and one draw needn't show every extreme that they name: `segments`: segment numbers never fall from one token to the next; every number is used, each names 1 to 768 consecutive tokens, and one names exactly 768.
All inputs are finite; a program needn't handle non-finite values.
Results may differ from a plain program's by a relative error of at most 0.014.
Values may be sent and summed in bfloat16 or wider, within the bound.
A program may use at most 128 MiB of HBM per device.

v0:
```python
import math
import jax
import jax.numpy as jnp
from jax import lax
from jax.sharding import PartitionSpec as P

QH = 32
KVH = 4
HD = 64
WINDOW = 128
epsilon = 1e-06
softcap = 50.0
rope_base = 10000.0


def from_behind(block, axis, distance):
    devices = range(lax.axis_size(axis))
    route = [(i - distance, i) for i in devices if i - distance in devices]
    return lax.ppermute(block, axis, route)


def rms_norm(inputs, scale_gain):
    values = inputs.astype(jnp.float32)
    return (
        values * lax.rsqrt(jnp.mean(values * values, axis=-1, keepdims=True) + epsilon) * scale_gain
    )


def rotate(inputs, positions):
    head_size = inputs.shape[-1]
    half_dim = head_size // 2
    frequency = jnp.exp(
        jnp.arange(half_dim, dtype=jnp.float32) * (-2.0 * math.log(rope_base) / head_size)
    )
    angles = positions.astype(jnp.float32)[:, None] * frequency[None, :]
    cosine_term = jnp.cos(angles)[:, None, :]
    sine_term = jnp.sin(angles)[:, None, :]
    lower_half = inputs[..., :half_dim]
    upper_half = inputs[..., half_dim:]
    return jnp.concatenate(
        [
            lower_half * cosine_term - upper_half * sine_term,
            upper_half * cosine_term + lower_half * sine_term,
        ],
        axis=-1,
    )


def attend_heads(block_queries, block_keys, block_values, seg_query, seg_key):
    query_count = block_queries.shape[0]
    key_count = block_keys.shape[0]
    head_span = QH // KVH * HD
    distance = (
        jnp.arange(query_count, dtype=jnp.int32)[:, None]
        + (key_count - query_count)
        - jnp.arange(key_count, dtype=jnp.int32)[None, :]
    )
    allowed = (distance >= 0) & (distance < WINDOW) & (seg_query[:, None] == seg_key[None, :])

    def one_head(head_index):
        query_head = lax.dynamic_slice_in_dim(
            block_queries, head_index * head_span, head_span, 1
        ).reshape(query_count, QH // KVH, HD)
        key_head = lax.dynamic_slice_in_dim(block_keys, head_index * HD, HD, 1)
        value_head = lax.dynamic_slice_in_dim(block_values, head_index * HD, HD, 1)
        scores = jnp.einsum("qgd,kd->gqk", query_head, key_head, preferred_element_type=jnp.float32)
        scores = softcap * jnp.tanh(scores / softcap)
        expanded = jnp.where(allowed[None], jnp.exp(scores), 0.0)
        weights = (expanded / jnp.sum(expanded, axis=-1, keepdims=True)).astype(jnp.bfloat16)
        head_out = jnp.einsum(
            "gqk,kd->qgd", weights, value_head, preferred_element_type=jnp.float32
        )
        return head_out.astype(jnp.bfloat16).reshape(query_count, head_span)

    per_head = lax.map(one_head, jnp.arange(KVH, dtype=jnp.int32))
    return per_head.transpose(1, 0, 2).reshape(query_count, KVH * head_span)


def body(
    hidden, segments, pre_gain, w_query, w_key, w_value, w_output, post_gain, final_gain, w_judge
):
    tok_rows = hidden.shape[1]
    dev_index = lax.axis_index("seq")
    row_first = dev_index * tok_rows
    own_rows = hidden[0]
    normed = rms_norm(own_rows, pre_gain[0]).astype(jnp.bfloat16)
    kv_count = normed.shape[0]
    queries = jnp.dot(
        normed,
        lax.all_gather(w_query[0], "seq", axis=0, tiled=True),
        preferred_element_type=jnp.float32,
    )
    key_rows = jnp.dot(
        normed,
        lax.all_gather(w_key[0], "seq", axis=0, tiled=True),
        preferred_element_type=jnp.float32,
    )
    val_rows = jnp.dot(
        normed,
        lax.all_gather(w_value[0], "seq", axis=0, tiled=True),
        preferred_element_type=jnp.float32,
    )
    query_positions = row_first + jnp.arange(tok_rows, dtype=jnp.int32)
    key_positions = row_first - (kv_count - tok_rows) + jnp.arange(kv_count, dtype=jnp.int32)
    queries = (
        (rotate(queries.reshape(tok_rows, QH, HD), query_positions) * (1.0 / math.sqrt(HD)))
        .astype(jnp.bfloat16)
        .reshape(tok_rows, QH * HD)
    )
    key_rows = (
        rotate(key_rows.reshape(kv_count, KVH, HD), key_positions)
        .astype(jnp.bfloat16)
        .reshape(kv_count, KVH * HD)
    )
    val_rows = val_rows.astype(jnp.bfloat16)
    earlier_keys, earlier_values = from_behind(
        (key_rows[tok_rows - WINDOW :], val_rows[tok_rows - WINDOW :]), "seq", 1
    )
    key_rows = jnp.concatenate([earlier_keys, key_rows], axis=0)
    val_rows = jnp.concatenate([earlier_values, val_rows], axis=0)
    seg_own = lax.dynamic_slice_in_dim(segments, row_first, tok_rows, 0)
    seg_prior = lax.dynamic_slice_in_dim(segments, jnp.maximum(row_first - WINDOW, 0), WINDOW, 0)
    seg_prior = jnp.where(dev_index > 0, seg_prior, -1)
    seg_keys = jnp.concatenate([seg_prior, seg_own], axis=0)
    block_rows = min(tok_rows, 512)

    def one_block(block_number):
        return attend_heads(queries, key_rows, val_rows, seg_own, seg_keys)

    attended = lax.map(one_block, jnp.arange(tok_rows // block_rows, dtype=jnp.int32)).reshape(
        tok_rows, QH * HD
    )
    projected = jnp.dot(
        attended,
        lax.all_gather(w_output[0], "seq", axis=0, tiled=True),
        preferred_element_type=jnp.float32,
    )
    updated = (own_rows.astype(jnp.float32) + rms_norm(projected, post_gain[0])).astype(
        jnp.bfloat16
    )
    closing = rms_norm(updated, final_gain[0]).astype(jnp.bfloat16)
    verdict = jnp.dot(closing, w_judge[0], preferred_element_type=jnp.float32)
    summed_verdict = lax.psum(verdict.astype(jnp.bfloat16), "member").astype(jnp.float32)
    return (updated[None], summed_verdict / lax.axis_size("member"))


def solution(mesh):
    return jax.shard_map(
        body,
        mesh=mesh,
        in_specs=(
            P("member", "seq", None),
            P(),
            P("member", None),
            P("member", "seq", None),
            P("member", "seq", None),
            P("member", "seq", None),
            P("member", "seq", None),
            P("member", None),
            P("member", None),
            P("member", None, None),
        ),
        out_specs=(P("member", "seq", None), P("seq", None)),
        check_vma=False,
    )
```

profile of v0, /device:TPU:2, one launch (start us, length us, event | category | flops | bytes accessed | tf_op | source)
XLA Modules:
  0.0 456.8 jit_solution(2094596954263053369)
XLA Ops:
  7.2 1.5 copy.24
  8.9 1.4 copy.25
  10.3 2.0 copy.27
  13.0 0.7 reduce
  13.7 0.7 reduce.1
  14.4 0.7 reduce.2
  15.2 0.8 dynamic_slice.19
  16.0 0.8 broadcast_select_fusion
  16.8 2.2 fusion.27
  19.2 71.9 %all-gather.9.cloned.1.call-done = bf16[1,2880,256]{2,0,1:T(2,128)(2,1)} async-done(((bf16[1,45,256]{2,0,1:T(2,128)(2,1)}), bf16[1,2880,256]{2,0,1:T(2,128)(2,1)}) %all-gather.9.cloned.1.call-update) | async-done | bytes 1474576 | tf_op jit(solution)/shard_map/all_gather | solution.py:100
  91.1 3.2 fusion.45
  94.4 0.7 copy-done.3
  95.1 2.1 collective-permute-start
  97.2 72.0 %all-gather.11.cloned.1.call-done = bf16[1,2880,256]{2,0,1:T(2,128)(2,1)} async-done(((bf16[1,45,256]{2,0,1:T(2,128)(2,1)}), bf16[1,2880,256]{2,0,1:T(2,128)(2,1)}) %all-gather.11.cloned.1.call-update) | async-done | bytes 1474576 | tf_op jit(solution)/shard_map/all_gather | solution.py:95
  169.2 7.3 %copy.34 = bf16[1,2880,256]{1,2,0:T(8,128)(2,1)} copy(bf16[1,2880,256]{2,0,1:T(2,128)(2,1)} %all-gather.11.cloned.1.call-done) | data formatting | bytes 2949120 | tf_op jit(solution)/shard_map/dot_general | solution.py:93
  176.6 2.5 fusion.56
  179.8 2.3 collective-permute-start.1
  182.1 0.9 pad_maximum_fusion
  183.0 0.8 copy.29
  183.8 3.0 collective-permute-done.1
  186.8 1.6 pad_maximum_fusion.1
  188.4 97.3 %all-gather.13.cloned.1.call-done = bf16[1,2880,2048]{2,0,1:T(2,128)(2,1)} async-done(((bf16[1,45,2048]{2,0,1:T(2,128)(2,1)}), bf16[1,2880,2048]{2,0,1:T(2,128)(2,1)}) %all-gather.13.cloned.1.call-update) | async-done | bytes 11796496 | tf_op jit(solution)/shard_map/all_gather | solution.py:90
  285.6 50.8 %copy.35 = bf16[1,2880,2048]{1,2,0:T(8,128)(2,1)} copy(bf16[1,2880,2048]{2,0,1:T(2,128)(2,1)} %all-gather.13.cloned.1.call-done) | data formatting | bytes 23592960 | tf_op jit(solution)/shard_map/dot_general | solution.py:88
  336.4 9.8 %fusion.54 = f32[384,32,64]{0,2,1:T(8,128)S(1)} fusion(bf16[32,64,2880]{2,1,0:T(8,128)(2,1)} %bitcast.102, bf16[1,384,2880]{1,2,0:T(8,128)(2,1)S(1)} %copy-done.1, f32[2880]{0:T(1024)S(1)} %reduce, f32[384]{0:T(512)S(1)} %copy-done.6), kind=kOutput, calls=%fused_computation.58 | convolution fusion | flops 4534272000 | bytes 17167104 | tf_op jit(solution)/shard_map/dot_general | solution.py:88
  346.7 1.5 fusion.33
  348.2 40.1 %while.18 = (s32[]{:T(128)}, bf16[4,384,512]{1,2,0:T(8,128)(2,1)}, s32[4]{0:T(128)S(1)}, bf16[512,256]{0,1:T(8,128)(2,1)}, bf16[512,256]{0,1:T(8,128)(2,1)}, /*i...) while((s32[]{:T(128)}, bf16[4,384,512]{1,2,0:T(8,128)(2,1)}, ...), condition=%wide.region_3.4_spmd.clone, body=%wide.region_1.3_spmd.clone.sunk | while | flops 418182144 | bytes 15693569 | solution.py:75
  349.5 1.0 constant_dynamic-slice_fusion.2
  351.5 3.0 fusion.71
  354.5 3.0 fusion.72
  357.5 0.8 constant_dynamic-update-slice_fusion.2
  359.5 1.0 constant_dynamic-slice_fusion.2
  361.5 3.0 fusion.71
  364.5 3.0 fusion.72
  367.5 0.8 constant_dynamic-update-slice_fusion.2
  369.5 1.0 constant_dynamic-slice_fusion.2
  371.5 3.0 fusion.71
  374.6 3.0 fusion.72
  377.5 0.8 constant_dynamic-update-slice_fusion.2
  379.6 1.0 constant_dynamic-slice_fusion.2
  381.6 3.0 fusion.71
  384.6 3.0 fusion.72
  387.6 0.8 constant_dynamic-update-slice_fusion.2
  388.4 10.0 %multiply_reduce_fusion = (f32[384]{0:T(512)S(1)}, f32[384,2880]{0,1:T(8,128)S(1)}) fusion(bf16[384,2048]{0,1:T(8,128)(2,1)} %bitcast.11, bf16[1,2048,2880]{2,1,0:T(8,128)(2,1)} %all-gather.15.cloned.1.call-done), kind=kOutput, calls=%fused_computation.41 | convolution fusion | flops 4532059648 | bytes 17794560 | tf_op jit(solution)/shard_map/dot_general | solution.py:133
  398.3 1.5 fusion.24
  399.8 1.3 copy-done.2
  401.2 2.1 fusion.50
  403.3 45.4 %all-reduce.2.cloned.1.call-done = bf16[384,128]{1,0:T(8,128)(2,1)} async-done(((bf16[384,128]{1,0:T(8,128)(2,1)}), bf16[384,128]{1,0:T(8,128)(2,1)}) %all-reduce.2.cloned.1.call-update) | async-done | bytes 98320 | tf_op jit(solution)/shard_map/psum | solution.py:143
  448.7 1.6 convert_multiply_fusion.3
  (47 shorter events, 5.8 us)
Async XLA Ops:
  7.2 394.0 %copy-start = (bf16[1,2880,128]{2,1,0:T(8,128)(2,1)S(1)}, bf16[1,2880,128]{2,1,0:T(8,128)(2,1)}, u32[]{:S(2)}) copy-start(bf16[1,2880,128]{2,1,0:T(8,128)(2,1)} %param.21) | copy-start | bytes 2211844
  7.2 83.9 %copy-start.1 = (bf16[1,384,2880]{1,2,0:T(8,128)(2,1)S(1)}, bf16[1,384,2880]{1,2,0:T(8,128)(2,1)}, u32[]{:S(2)}) copy-start(bf16[1,384,2880]{1,2,0:T(8,128)(2,1)} %param.12) | copy-start | bytes 6635524
  7.2 83.9 %all-gather.9.cloned.1.call-start = ((), (), s32[]{:S(2)}) async-start(), calls=%async_computation.1 | async-start | bytes 2995200 | tf_op jit(solution)/shard_map/all_gather | solution.py:100
  8.8 160.4 %all-gather.11.cloned.1.call-start = ((), (), s32[]{:S(2)}) async-start(), calls=%async_computation.2 | async-start | bytes 2995200 | tf_op jit(solution)/shard_map/all_gather | solution.py:95
  10.3 275.4 %all-gather.13.cloned.1.call-start = ((), (), s32[]{:S(2)}) async-start(), calls=%async_computation.3 | async-start | bytes 23961600 | tf_op jit(solution)/shard_map/all_gather | solution.py:90
  12.3 376.0 %all-gather.15.cloned.1.call-start = ((), (), s32[]{:S(2)}) async-start(), calls=%async_computation.4 | async-start | bytes 12247040 | tf_op jit(solution)/shard_map/all_gather | solution.py:135
  12.9 435.8 %all-reduce.2.cloned.1.call-start = ((), (), s32[]{:S(2)}) async-start(), calls=%async_computation | async-start | bytes 196608 | tf_op jit(solution)/shard_map/psum | solution.py:143
  19.0 157.6 %copy-start.5 = (f32[384]{0:T(512)}, f32[384]{0:T(512)S(1)}, u32[]{:S(2)}) copy-start(f32[384]{0:T(512)S(1)} %add_rsqrt_fusion.2) | copy-start | bytes 4612
  94.4 0.7 copy-start.3
  95.1 87.0 %collective-permute-start = (bf16[128,256]{1,0:T(8,128)(2,1)S(1)}, bf16[128,256]{1,0:T(8,128)(2,1)}, u32[]{:S(2)}, u32[]{:S(2)}) collective-permute-start(bf16[128,256]{1,0:T(8,128)(2,1)S(1)} %slice.28), channel_id=1, source_target_pairs={{0,1},{1,2},{2,3},{3,4},{4,5},{5,6},{6,7},{7,8},{8,9},{9,10},{10,1... | collective-permute-start | bytes 196616 | tf_op jit(solution)/shard_map/ppermute | solution.py:19
  176.5 5.5 %copy-start.4 = (bf16[384,256]{1,0:T(8,128)(2,1)S(1)}, bf16[384,256]{1,0:T(8,128)(2,1)}, u32[]{:S(2)}) copy-start(bf16[384,256]{1,0:T(8,128)(2,1)} %copy-done.3) | copy-start | bytes 589828
  179.8 7.0 %collective-permute-start.1 = (bf16[128,256]{0,1:T(8,128)(2,1)}, bf16[128,256]{0,1:T(8,128)(2,1)}, u32[]{:S(2)}, u32[]{:S(2)}) collective-permute-start(bf16[128,256]{0,1:T(8,128)(2,1)} %bitcast.5), channel_id=1, source_target_pairs={{0,1},{1,2},{2,3},{3,4},{4,5},{5,6},{6,7},{7,8},{8,9},{9,10},{10,1... | collective-permute-start | bytes 196616 | tf_op jit(solution)/shard_map/ppermute | solution.py:19
  188.4 148.1 %copy-start.6 = (f32[384]{0:T(512)S(1)}, f32[384]{0:T(512)}, u32[]{:S(2)}) copy-start(f32[384]{0:T(512)} %copy-done.5) | copy-start | bytes 4612
  399.8 1.4 copy-start.2
Sparse Core Ops, SparseCore 0:
  11.3 79.8 all-gather.8
  93.8 75.3 all-gather.10
  172.0 113.6 all-gather.12
  288.2 85.5 all-gather.14
  403.4 45.2 all-reduce.1
where the time goes:
time: 460 us; the launch traced here: 457 us
  waiting for transfers between devices  290 us (63%)
  local copies, waits for them, and re-layouts  77 us (17%)
  matrix products  51.6 us (11%)
  other arithmetic  14.2 us (3%)
  between operations  14 us (3%)
  loops' own time  5.31 us (1%)
  starting transfers between devices  4.61 us (1%)
    all_gather x1, waiting for transfers between devices, body(): lax.all_gather(w_query[0], 'seq', axis=0, tiled=True)  97.3 us
    all_gather x1, waiting for transfers between devices, body(): lax.all_gather(w_key[0], 'seq', axis=0, tiled=True)  72 us
    all_gather x1, waiting for transfers between devices, body(): lax.all_gather(w_value[0], 'seq', axis=0, tiled=True)  71.9 us
    dot_general x1, local copies, waits for them, and re-layouts, body(): jnp.dot(normed, lax.all_gather(w_query[0], 'seq', axis=0, tiled=True), pr...  50.8 us
    psum x1, waiting for transfers between devices, body(): lax.psum(verdict.astype(jnp.bfloat16), 'member').astype(jnp.float32)  45.4 us
    dot_general x4, matrix products, one_head(): jnp.einsum('qgd,kd->gqk', query_head, key_head, preferred_element_type=jn...  12.1 us
    dot_general x4, matrix products, one_head(): jnp.einsum('gqk,kd->qgd', weights, value_head, preferred_element_type=jnp...  11.9 us
    dot_general x1, matrix products, body(): jnp.dot(attended, lax.all_gather(w_output[0], 'seq', axis=0, tiled=True),...  9.97 us
  transfers between devices with their start and end apart: 7, of which 5 were waited for; matrix products, arithmetic and copies ran while one was open for 27% of the time, Pallas kernels for 0%

commit v1 on v0

--- a/solution.py
+++ b/solution.py
@@ -87,7 +87,9 @@
     kv_count = normed.shape[0]
     queries = jnp.dot(
         normed,
-        lax.all_gather(w_query[0], "seq", axis=0, tiled=True),
+        jnp.concatenate(
+            lax.all_to_all(jnp.stack([w_query[0]] * lax.axis_size("seq")), "seq", 0, 0), axis=0
+        ),
         preferred_element_type=jnp.float32,
     )
     key_rows = jnp.dot(

time: 460 us -> 480 us (1.043)
  waiting for transfers between devices: 290 us -> 322 us
  local copies, waits for them, and re-layouts: 77 us -> 58.4 us
  starting transfers between devices: 4.61 us -> 16.7 us
    all_gather x1 -> x0, waiting for transfers between devices: 97.3 us -> none  [body(): lax.all_gather(w_query[0], 'seq', axis=0, tiled=True)]
    all_to_all x0 -> x1, waiting for transfers between devices: none -> 52.2 us  [body(): lax.all_to_all(jnp.stack([w_query[0]] * lax.axis_size('seq')), 'seq', 0, 0)]
    all_gather x1, waiting for transfers between devices: 71.9 us -> 120 us  [body(): lax.all_gather(w_value[0], 'seq', axis=0, tiled=True)]
    dot_general x1, local copies, waits for them, and re-layouts: 50.8 us -> 16.4 us  [body(): jnp.dot(normed, jnp.concatenate(lax.all_to_all(jnp.stack([w_query[0]] * l...]
    all_gather x1, waiting for transfers between devices: 72 us -> 98.9 us  [body(): lax.all_gather(w_key[0], 'seq', axis=0, tiled=True)]
    all_to_all x0 -> x1, starting transfers between devices: none -> 12.3 us  [body(): lax.all_to_all(jnp.stack([w_query[0]] * lax.axis_size('seq')), 'seq', 0, 0)]
    reshape x0 -> x1, local copies, waits for them, and re-layouts: none -> 12.3 us  [body(): jnp.concatenate(lax.all_to_all(jnp.stack([w_query[0]] * lax.axis_size('se...]
    another operation x0 -> x1, local copies, waits for them, and re-layouts: none -> 7.06 us  [body(): jnp.stack([w_query[0]] * lax.axis_size('seq'))]
  transfers between devices with their start and end apart: 7 -> 7, of which waited for: 5 -> 5; matrix products, arithmetic and copies ran while one was open for 27% -> 20% of each run, Pallas kernels for 0% -> 0%
where the time goes in v1:
time: 480 us; the launch traced here: 478 us
  waiting for transfers between devices  322 us (67%)
  local copies, waits for them, and re-layouts  58.4 us (12%)
  matrix products  51.4 us (11%)
  starting transfers between devices  16.7 us (3%)
  between operations  14 us (3%)
  other arithmetic  10.4 us (2%)
  loops' own time  5.3 us (1%)
    all_gather x1, waiting for transfers between devices, body(): lax.all_gather(w_value[0], 'seq', axis=0, tiled=True)  120 us
    all_gather x1, waiting for transfers between devices, body(): lax.all_gather(w_key[0], 'seq', axis=0, tiled=True)  98.9 us
    all_to_all x1, waiting for transfers between devices, body(): lax.all_to_all(jnp.stack([w_query[0]] * lax.axis_size('seq')), 'seq', 0, 0)  52.2 us
    psum x1, waiting for transfers between devices, body(): lax.psum(verdict.astype(jnp.bfloat16), 'member').astype(jnp.float32)  47.2 us
    dot_general x1, local copies, waits for them, and re-layouts, body(): jnp.dot(normed, jnp.concatenate(lax.all_to_all(jnp.stack([w_query[0]] * l...  16.4 us
    all_to_all x1, starting transfers between devices, body(): lax.all_to_all(jnp.stack([w_query[0]] * lax.axis_size('seq')), 'seq', 0, 0)  12.3 us
    reshape x1, local copies, waits for them, and re-layouts, body(): jnp.concatenate(lax.all_to_all(jnp.stack([w_query[0]] * lax.axis_size('se...  12.3 us
    dot_general x4, matrix products, one_head(): jnp.einsum('qgd,kd->gqk', query_head, key_head, preferred_element_type=jn...  12.1 us
  transfers between devices with their start and end apart: 7, of which 5 were waited for; matrix products, arithmetic and copies ran while one was open for 20% of the time, Pallas kernels for 0%

profile of v1, /device:TPU:2, one launch (start us, length us, event | category | flops | bytes accessed | tf_op | source)
XLA Modules:
  0.0 478.0 jit_solution(7381313044075834169)
XLA Ops:
  7.2 7.1 %stack.3 = bf16[64,45,2048]{2,1,0:T(8,128)(2,1)} broadcast(bf16[45,2048]{1,0:T(8,128)(2,1)} %bitcast.107), dimensions={1,2} | broadcast | bytes 11980800 | tf_op jit(solution)/shard_map/stack | solution.py:91
  14.3 12.3 %all-to-all-start = ((bf16[64,45,2048]{2,1,0:T(8,128)(2,1)}), bf16[64,45,2048]{2,1,0:T(8,128)(2,1)}, u32[]{:S(2)}, u32[]{:S(2)}) async-start(bf16[64,45,2048]{2,1,0:T(8,128)(2,1)} %stack.3), calls=%async_computation | async-start | bytes 25165824 | tf_op jit(solution)/shard_map/all_to_all | solution.py:91
  26.7 0.7 copy.27
  27.4 0.7 copy.28
  28.2 0.7 all-gather.11.cloned.1.call-update
  29.1 0.8 dynamic_slice.19
  29.8 0.8 broadcast_select_fusion
  31.5 120.2 %all-gather.7.cloned.1.call-done = bf16[1,2880,256]{2,0,1:T(2,128)(2,1)} async-done(((bf16[1,45,256]{2,0,1:T(2,128)(2,1)}), bf16[1,2880,256]{2,0,1:T(2,128)(2,1)}) %all-gather.7.cloned.1.call-update) | async-done | bytes 1474576 | tf_op jit(solution)/shard_map/all_gather | solution.py:102
  151.7 3.2 fusion.45
  154.9 0.7 copy-done.3
  155.6 2.1 collective-permute-start
  157.7 98.9 %all-gather.9.cloned.1.call-done = bf16[1,2880,256]{2,0,1:T(2,128)(2,1)} async-done(((bf16[1,45,256]{2,0,1:T(2,128)(2,1)}), bf16[1,2880,256]{2,0,1:T(2,128)(2,1)}) %all-gather.9.cloned.1.call-update) | async-done | bytes 1474576 | tf_op jit(solution)/shard_map/all_gather | solution.py:97
  256.6 7.3 %copy.35 = bf16[1,2880,256]{1,2,0:T(8,128)(2,1)} copy(bf16[1,2880,256]{2,0,1:T(2,128)(2,1)} %all-gather.9.cloned.1.call-done) | data formatting | bytes 2949120 | tf_op jit(solution)/shard_map/dot_general | solution.py:95
  263.9 2.5 fusion.56
  266.5 0.6 slice.31
  267.1 2.1 collective-permute-start.1
  269.3 0.9 pad_maximum_fusion
  270.1 0.9 copy.31
  271.0 2.5 collective-permute-done.1
  273.5 1.6 pad_maximum_fusion.1
  275.1 52.2 %all-to-all-done = bf16[64,45,2048]{2,1,0:T(8,128)(2,1)} async-done(((bf16[64,45,2048]{2,1,0:T(8,128)(2,1)}), bf16[64,45,2048]{2,1,0:T(8,128)(2,1)}, u32[]{:S(2)}, u32[]{:S(2)}) %all-to-all-start) | async-done | bytes 11796512 | tf_op jit(solution)/shard_map/all_to_all | solution.py:91
  327.3 12.3 %reshape.157 = bf16[2880,2048]{1,0:T(8,128)(2,1)} reshape(bf16[64,45,2048]{2,1,0:T(8,128)(2,1)} %all-to-all-done) | data formatting | bytes 23592960 | tf_op jit(solution)/shard_map/reshape | solution.py:90
  339.6 16.4 %copy.30 = bf16[2048,2880]{1,0:T(8,128)(2,1)} copy(bf16[2048,2880]{0,1:T(8,128)(2,1)} %bitcast.99) | data formatting | bytes 23592960 | tf_op jit(solution)/shard_map/dot_general | solution.py:88
  356.0 9.7 %fusion.54 = f32[384,32,64]{0,2,1:T(8,128)S(1)} fusion(bf16[32,64,2880]{2,1,0:T(8,128)(2,1)} %bitcast.100, bf16[1,384,2880]{1,2,0:T(8,128)(2,1)S(1)} %copy-done.1, f32[2880]{0:T(1024)S(1)} %reduce, f32[384]{0:T(512)S(1)} %copy-done.11), kind=kOutput, calls=%fused_computation.58 | convolution fusion | flops 4534272000 | bytes 17167104 | tf_op jit(solution)/shard_map/dot_general | solution.py:88
  366.2 1.5 fusion.33
  367.7 40.1 %while.18 = (s32[]{:T(128)}, bf16[4,384,512]{1,2,0:T(8,128)(2,1)}, s32[4]{0:T(128)S(1)}, bf16[512,256]{0,1:T(8,128)(2,1)}, bf16[512,256]{0,1:T(8,128)(2,1)}, /*i...) while((s32[]{:T(128)}, bf16[4,384,512]{1,2,0:T(8,128)(2,1)}, ...), condition=%wide.region_3.4_spmd.clone, body=%wide.region_1.3_spmd.clone.sunk | while | flops 418182144 | bytes 15693569 | solution.py:75
  368.9 1.1 constant_dynamic-slice_fusion.2
  371.0 3.0 fusion.71
  374.0 3.0 fusion.72
  377.0 0.8 constant_dynamic-update-slice_fusion.2
  379.0 1.0 constant_dynamic-slice_fusion.2
  381.0 3.0 fusion.71
  384.0 3.0 fusion.72
  387.0 0.8 constant_dynamic-update-slice_fusion.2
  389.0 1.0 constant_dynamic-slice_fusion.2
  391.0 3.0 fusion.71
  394.0 3.0 fusion.72
  397.0 0.8 constant_dynamic-update-slice_fusion.2
  399.0 1.0 constant_dynamic-slice_fusion.2
  401.0 3.0 fusion.71
  404.1 3.0 fusion.72
  407.0 0.8 constant_dynamic-update-slice_fusion.2
  407.8 10.0 %multiply_reduce_fusion = (f32[384]{0:T(512)S(1)}, f32[384,2880]{0,1:T(8,128)S(1)}) fusion(bf16[384,2048]{0,1:T(8,128)(2,1)} %bitcast.12, bf16[1,2048,2880]{2,1,0:T(8,128)(2,1)} %all-gather.11.cloned.1.call-done), kind=kOutput, calls=%fused_computation.41 | convolution fusion | flops 4532059648 | bytes 17794560 | tf_op jit(solution)/shard_map/dot_general | solution.py:135
  417.8 1.5 fusion.24
  419.3 1.3 copy-done.2
  420.7 2.1 fusion.50
  422.8 47.2 %all-reduce.2.cloned.1.call-done = bf16[384,128]{1,0:T(8,128)(2,1)} async-done(((bf16[384,128]{1,0:T(8,128)(2,1)}), bf16[384,128]{1,0:T(8,128)(2,1)}) %all-reduce.2.cloned.1.call-update) | async-done | bytes 98320 | tf_op jit(solution)/shard_map/psum | solution.py:145
  469.9 1.6 convert_multiply_fusion.3
  (57 shorter events, 5.3 us)
Async XLA Ops:
  7.2 413.5 %copy-start = (bf16[1,2880,128]{2,1,0:T(8,128)(2,1)S(1)}, bf16[1,2880,128]{2,1,0:T(8,128)(2,1)}, u32[]{:S(2)}) copy-start(bf16[1,2880,128]{2,1,0:T(8,128)(2,1)} %param.21) | copy-start | bytes 2211844
  14.2 12.4 %copy-start.5 = (bf16[1,45,256]{2,1,0:T(8,128)(2,1)S(1)}, bf16[1,45,256]{2,1,0:T(8,128)(2,1)}, u32[]{:S(2)}) copy-start(bf16[1,45,256]{2,1,0:T(8,128)(2,1)} %param.17) | copy-start | bytes 69124
  14.2 13.2 %copy-start.6 = (bf16[1,45,256]{2,1,0:T(8,128)(2,1)S(1)}, bf16[1,45,256]{2,1,0:T(8,128)(2,1)}, u32[]{:S(2)}) copy-start(bf16[1,45,256]{2,1,0:T(8,128)(2,1)} %param.16) | copy-start | bytes 69124
  14.2 14.7 %copy-start.7 = (f32[1,2880]{1,0:T(1,128)S(1)}, f32[1,2880]{1,0:T(1,128)}, u32[]{:S(2)}) copy-start(f32[1,2880]{1,0:T(1,128)} %param.14) | copy-start | bytes 34564
  14.2 14.7 %copy-start.8 = (f32[1,2880]{1,0:T(1,128)S(1)}, f32[1,2880]{1,0:T(1,128)}, u32[]{:S(2)}) copy-start(f32[1,2880]{1,0:T(1,128)} %param.19) | copy-start | bytes 34564
  14.3 14.8 %copy-start.9 = (f32[1,2880]{1,0:T(1,128)S(1)}, f32[1,2880]{1,0:T(1,128)}, u32[]{:S(2)}) copy-start(f32[1,2880]{1,0:T(1,128)} %param.20) | copy-start | bytes 34564
  14.3 16.4 %copy-start.1 = (bf16[1,384,2880]{1,2,0:T(8,128)(2,1)S(1)}, bf16[1,384,2880]{1,2,0:T(8,128)(2,1)}, u32[]{:S(2)}) copy-start(bf16[1,384,2880]{1,2,0:T(8,128)(2,1)} %param.12) | copy-start | bytes 6635524
  14.3 313.0 %all-to-all-start = ((bf16[64,45,2048]{2,1,0:T(8,128)(2,1)}), bf16[64,45,2048]{2,1,0:T(8,128)(2,1)}, u32[]{:S(2)}, u32[]{:S(2)}) async-start(bf16[64,45,2048]{2,1,0:T(8,128)(2,1)} %stack.3), calls=%async_computation | async-start | bytes 25165824 | tf_op jit(solution)/shard_map/all_to_all | solution.py:91
  26.6 125.1 %all-gather.7.cloned.1.call-start = ((), (), s32[]{:S(2)}) async-start(), calls=%async_computation.2 | async-start | bytes 2995200 | tf_op jit(solution)/shard_map/all_gather | solution.py:102
  27.4 229.3 %all-gather.9.cloned.1.call-start = ((), (), s32[]{:S(2)}) async-start(), calls=%async_computation.3 | async-start | bytes 2995200 | tf_op jit(solution)/shard_map/all_gather | solution.py:97
  28.1 379.7 %all-gather.11.cloned.1.call-start = ((), (), s32[]{:S(2)}) async-start(), calls=%async_computation.4 | async-start | bytes 12247040 | tf_op jit(solution)/shard_map/all_gather | solution.py:137
  28.8 441.1 %all-reduce.2.cloned.1.call-start = ((), (), s32[]{:S(2)}) async-start(), calls=%async_computation.1 | async-start | bytes 196608 | tf_op jit(solution)/shard_map/psum | solution.py:145
  31.2 232.7 %copy-start.10 = (f32[384]{0:T(512)}, f32[384]{0:T(512)S(1)}, u32[]{:S(2)}) copy-start(f32[384]{0:T(512)S(1)} %add_rsqrt_fusion.2) | copy-start | bytes 4612
  154.9 0.7 copy-start.3
  155.6 113.7 %collective-permute-start = (bf16[128,256]{1,0:T(8,128)(2,1)S(1)}, bf16[128,256]{1,0:T(8,128)(2,1)}, u32[]{:S(2)}, u32[]{:S(2)}) collective-permute-start(bf16[128,256]{1,0:T(8,128)(2,1)S(1)} %slice.28), channel_id=1, source_target_pairs={{0,1},{1,2},{2,3},{3,4},{4,5},{5,6},{6,7},{7,8},{8,9},{9,10},{10,1... | collective-permute-start | bytes 196616 | tf_op jit(solution)/shard_map/ppermute | solution.py:19
  263.9 5.4 %copy-start.4 = (bf16[384,256]{1,0:T(8,128)(2,1)S(1)}, bf16[384,256]{1,0:T(8,128)(2,1)}, u32[]{:S(2)}) copy-start(bf16[384,256]{1,0:T(8,128)(2,1)} %copy-done.3) | copy-start | bytes 589828
  267.1 6.4 %collective-permute-start.1 = (bf16[128,256]{0,1:T(8,128)(2,1)}, bf16[128,256]{0,1:T(8,128)(2,1)}, u32[]{:S(2)}, u32[]{:S(2)}) collective-permute-start(bf16[128,256]{0,1:T(8,128)(2,1)} %bitcast.5), channel_id=1, source_target_pairs={{0,1},{1,2},{2,3},{3,4},{4,5},{5,6},{6,7},{7,8},{8,9},{9,10},{10,1... | collective-permute-start | bytes 196616 | tf_op jit(solution)/shard_map/ppermute | solution.py:19
  339.6 16.4 %copy-start.11 = (f32[384]{0:T(512)S(1)}, f32[384]{0:T(512)}, u32[]{:S(2)}) copy-start(f32[384]{0:T(512)} %copy-done.10) | copy-start | bytes 4612
  419.3 1.4 copy-start.2
Sparse Core Ops, SparseCore 0:
  30.7 120.9 all-gather.6
  154.4 102.1 all-gather.8
  259.3 118.9 all-gather.10
  422.9 46.9 all-reduce.1
